TPU v7x, 32 devices: a whole 2x2x4 slice. The times are simulated.
32 devices in a mesh: dp: 16 (over z, y, core), tensor: 2 (over x).
Axes of the slice: x: 2, y: 2, z: 4, core: 2. Of those that a mesh axis runs over, the one named last changes fastest.
Arguments:
- layer_input: bfloat16 [10240, 1024], P('dp'), may hold values from -8 to 8
- output_grad: bfloat16 [10240, 1024], P('dp'), may hold values from -6 to 6
- attn_gain: float32 [1024], replicated, may hold values from 0.5 to 1.5
- attn_shift: float32 [1024], replicated, may hold values from -3 to 3
- mlp_gain: float32 [1024], replicated, may hold values from 0.5 to 1.5
- mlp_shift: float32 [1024], replicated, may hold values from -3 to 3
- qkv_weight: bfloat16 [1024, 3072], P(None, 'tensor'), may hold values from -1 to 1
- qkv_bias: float32 [3072], P('tensor'), may hold values from -3 to 3
- dense_weight: bfloat16 [1024, 1024], P('tensor'), may hold values from -0.75 to 0.75
- dense_bias: float32 [1024], replicated, may hold values from -3 to 3
- expand_weight: bfloat16 [1024, 4096], P(None, 'tensor'), may hold values from -0.1875 to 0.1875
- expand_bias: float32 [4096], P('tensor'), may hold values from -3 to 3
- contract_weight: bfloat16 [4096, 1024], P('tensor'), may hold values from -0.09375 to 0.09375
- contract_bias: float32 [1024], replicated, may hold values from -3 to 3
Outputs:
- layer_output: bfloat16 [10240, 1024], P('dp')
- input_grad: bfloat16 [10240, 1024], P('dp')
- attn_gain_grad: float32 [1024], replicated
- attn_shift_grad: float32 [1024], replicated
- mlp_gain_grad: float32 [1024], replicated
- mlp_shift_grad: float32 [1024], replicated
- qkv_weight_grad: float32 [1024, 3072], P('dp', 'tensor')
- qkv_bias_grad: float32 [3072], P('tensor')
- dense_weight_grad: float32 [1024, 1024], P('tensor', 'dp')
- dense_bias_grad: float32 [1024], replicated
- expand_weight_grad: float32 [1024, 4096], P('dp', 'tensor')
- expand_bias_grad: float32 [4096], P('tensor')
- contract_weight_grad: float32 [4096, 1024], P('tensor', 'dp')
- contract_bias_grad: float32 [1024], replicated
All inputs are finite; a program needn't handle non-finite values.
Results may differ from a plain program's by a relative error of at most 0.0085.
The roundings to bfloat16 on the way count: a program that leaves them out, or rounds other values in their place, can miss the bound.
Values sent between devices are 32-bit elements; how exact they have to be, the bound alone decides.
A program may use at most 192 MiB of HBM per device.

v0:
```python
import jax
import jax.numpy as jnp
from jax import lax
from jax.sharding import PartitionSpec as P

HEAD_DIM = 64
ROT = 16


NORM_EPS = 1e-05
SQRT_HALF = 0.7071067811865476
INV_ROOT_TWO_PI = 0.3989422804014327


def normalize(values):
    center = values - jnp.mean(values, axis=1, keepdims=True)
    inverse = lax.rsqrt(jnp.mean(center * center, axis=1, keepdims=True) + NORM_EPS)
    return (center * inverse, inverse)


def norm_backward(norm_grad, scaling, unit_rows, inverse):
    scaled = norm_grad * scaling
    return inverse * (
        scaled
        - jnp.mean(scaled, axis=1, keepdims=True)
        - unit_rows * jnp.mean(scaled * unit_rows, axis=1, keepdims=True)
    )


def rotary_tables(length):
    halfway = ROT // 2
    frequency = 10000.0 ** (-2.0 * jnp.arange(halfway, dtype=jnp.float32) / ROT)
    angles = jnp.arange(length, dtype=jnp.float32)[:, None] * frequency[None, :]
    return (jnp.cos(angles)[:, None, :], jnp.sin(angles)[:, None, :])


def rotate(vectors, cosine, sine_table, direction):
    halfway = ROT // 2
    first_half = vectors[..., :halfway]
    second_half = vectors[..., halfway:ROT]
    return jnp.concatenate(
        [
            first_half * cosine - direction * second_half * sine_table,
            second_half * cosine + direction * first_half * sine_table,
            vectors[..., ROT:],
        ],
        axis=-1,
    )


def gelu_value(hidden_in):
    return 0.5 * hidden_in * (1.0 + lax.erf(hidden_in * SQRT_HALF))


def gelu_slope(hidden_in):
    return (
        0.5 * (1.0 + lax.erf(hidden_in * SQRT_HALF))
        + hidden_in * jnp.exp(-0.5 * hidden_in * hidden_in) * INV_ROOT_TWO_PI
    )


def column_products(left_cols, right_rows):
    return lax.dot_general(
        left_cols, right_rows, (((0,), (0,)), ((), ())), preferred_element_type=jnp.float32
    )


def masked_scores(queries, keys_rot):
    length = queries.shape[0]
    scores = jnp.einsum(
        "qhd,khd->hqk", queries, keys_rot, preferred_element_type=jnp.float32
    ) * HEAD_DIM ** (-0.5)
    causal = jnp.arange(length)[:, None] >= jnp.arange(length)[None, :]
    return jnp.where(causal[None], scores, -jnp.inf)


def body(
    layer_input,
    output_grad,
    attn_gain,
    attn_shift,
    mlp_gain,
    mlp_shift,
    qkv_weight,
    qkv_bias,
    dense_weight,
    dense_bias,
    expand_weight,
    expand_bias,
    contract_weight,
    contract_bias,
):
    length = layer_input.shape[0]
    heads_here = qkv_weight.shape[1] // (3 * HEAD_DIM)
    qkv_cols = qkv_weight.shape[1]
    ff_here = expand_weight.shape[1]
    wide_input = layer_input.astype(jnp.float32)
    unit_rows, inverse = normalize(wide_input)
    ln_attn = (unit_rows * attn_gain + attn_shift).astype(jnp.bfloat16)
    ln_mlp = (unit_rows * mlp_gain + mlp_shift).astype(jnp.bfloat16)
    cosine, sine_table = rotary_tables(length)
    mixed = (jnp.dot(ln_attn, qkv_weight, preferred_element_type=jnp.float32) + qkv_bias).reshape(
        length, heads_here, 3, HEAD_DIM
    )
    queries = rotate(mixed[:, :, 0], cosine, sine_table, 1.0).astype(jnp.bfloat16)
    keys_rot = rotate(mixed[:, :, 1], cosine, sine_table, 1.0).astype(jnp.bfloat16)
    values_low = mixed[:, :, 2].astype(jnp.bfloat16)
    scores = masked_scores(queries, keys_rot)
    row_max = jnp.max(scores, axis=2, keepdims=True)
    log_total = row_max + jnp.log(jnp.sum(jnp.exp(scores - row_max), axis=2, keepdims=True))
    probs_low = jnp.exp(scores - log_total).astype(jnp.bfloat16)
    context = jnp.einsum("hqk,khd->qhd", probs_low, values_low, preferred_element_type=jnp.float32)
    context = context.astype(jnp.bfloat16).reshape(length, heads_here * HEAD_DIM)
    hidden = jnp.dot(ln_mlp, expand_weight, preferred_element_type=jnp.float32) + expand_bias
    active = gelu_value(hidden).astype(jnp.bfloat16)
    partial_out = jnp.dot(context, dense_weight, preferred_element_type=jnp.float32) + jnp.dot(
        active, contract_weight, preferred_element_type=jnp.float32
    )
    branches = lax.psum(partial_out, "tensor")
    layer_output = (wide_input + branches + dense_bias + contract_bias).astype(jnp.bfloat16)
    upstream_f = output_grad.astype(jnp.float32)
    bias_term = jnp.sum(upstream_f, axis=0)
    hidden_grad = jnp.dot(
        output_grad, contract_weight.T, preferred_element_type=jnp.float32
    ) * gelu_slope(hidden)
    expand_bias_term = jnp.sum(hidden_grad, axis=0)
    hidden_low = hidden_grad.astype(jnp.bfloat16)
    mlp_norm_part = jnp.dot(hidden_low, expand_weight.T, preferred_element_type=jnp.float32)
    context_grad = jnp.dot(output_grad, dense_weight.T, preferred_element_type=jnp.float32)
    context_grad = context_grad.astype(jnp.bfloat16).reshape(length, heads_here, HEAD_DIM)
    probs = jnp.exp(masked_scores(queries, keys_rot) - log_total)
    probs_again = probs.astype(jnp.bfloat16)
    value_grad = jnp.einsum(
        "hqk,qhd->khd", probs_again, context_grad, preferred_element_type=jnp.float32
    )
    prob_grad = jnp.einsum(
        "qhd,khd->hqk", context_grad, values_low, preferred_element_type=jnp.float32
    )
    row_delta = jnp.sum(probs * prob_grad, axis=2, keepdims=True)
    score_grad = (probs * (prob_grad - row_delta) * HEAD_DIM ** (-0.5)).astype(jnp.bfloat16)
    query_grad = jnp.einsum(
        "hqk,khd->qhd", score_grad, keys_rot, preferred_element_type=jnp.float32
    )
    key_grad = jnp.einsum("hqk,qhd->khd", score_grad, queries, preferred_element_type=jnp.float32)
    query_grad = rotate(query_grad, cosine, sine_table, -1.0)
    key_grad = rotate(key_grad, cosine, sine_table, -1.0)
    mixed_grad = jnp.stack([query_grad, key_grad, value_grad], axis=2).reshape(length, qkv_cols)
    qkv_bias_term = jnp.sum(mixed_grad, axis=0)
    mixed_low = mixed_grad.astype(jnp.bfloat16)
    attn_norm_part = jnp.dot(mixed_low, qkv_weight.T, preferred_element_type=jnp.float32)
    both_summed = lax.psum_scatter(
        jnp.concatenate(
            [
                jnp.concatenate(
                    [column_products(ln_attn, mixed_low), column_products(output_grad, context)],
                    axis=1,
                ),
                jnp.concatenate(
                    [column_products(ln_mlp, hidden_low), column_products(output_grad, active)],
                    axis=1,
                ),
            ],
            axis=1,
        ),
        "dp",
        scatter_dimension=0,
        tiled=True,
    )
    attn_width = qkv_cols + heads_here * HEAD_DIM
    attn_summed = both_summed[:, :attn_width]
    mlp_summed = both_summed[:, attn_width:]
    attn_norm_grad, mlp_norm_grad = lax.psum((attn_norm_part, mlp_norm_part), "tensor")
    vectors = jnp.stack(
        [
            jnp.sum(attn_norm_grad * unit_rows, axis=0),
            jnp.sum(attn_norm_grad, axis=0),
            jnp.sum(mlp_norm_grad * unit_rows, axis=0),
            jnp.sum(mlp_norm_grad, axis=0),
            bias_term,
        ]
    )
    input_back = norm_backward(attn_norm_grad, attn_gain, unit_rows, inverse) + norm_backward(
        mlp_norm_grad, mlp_gain, unit_rows, inverse
    )
    input_grad = (upstream_f + input_back).astype(jnp.bfloat16)
    vectors, qkv_bias_grad, expand_bias_grad = lax.psum(
        (vectors, qkv_bias_term, expand_bias_term), "dp"
    )
    qkv_weight_grad = attn_summed[:, :qkv_cols]
    dense_weight_grad = attn_summed[:, qkv_cols:].T
    expand_weight_grad = mlp_summed[:, :ff_here]
    contract_weight_grad = mlp_summed[:, ff_here:].T
    return (
        layer_output,
        input_grad,
        vectors[0],
        vectors[1],
        vectors[2],
        vectors[3],
        qkv_weight_grad,
        qkv_bias_grad,
        dense_weight_grad,
        vectors[4],
        expand_weight_grad,
        expand_bias_grad,
        contract_weight_grad,
        vectors[4],
    )


def solution(mesh):
    in_specs = (
        P("dp", None),
        P("dp", None),
        P(),
        P(),
        P(),
        P(),
        P(None, "tensor"),
        P("tensor"),
        P("tensor", None),
        P(),
        P(None, "tensor"),
        P("tensor"),
        P("tensor", None),
        P(),
    )
    out_specs = (
        P("dp", None),
        P("dp", None),
        P(),
        P(),
        P(),
        P(),
        P("dp", "tensor"),
        P("tensor"),
        P("tensor", "dp"),
        P(),
        P("dp", "tensor"),
        P("tensor"),
        P("tensor", "dp"),
        P(),
    )
    return jax.shard_map(body, mesh=mesh, in_specs=in_specs, out_specs=out_specs, check_vma=False)
```

profile of v0, /device:TPU:0, one launch (start us, length us, event | category | flops | bytes accessed | tf_op | source)
XLA Modules:
  0.0 437.4 jit_solution(18004381641851076231)
XLA Ops:
  8.0 0.0 all-reduce.4.cloned.1.call-start
  8.1 0.1 iota_compare_fusion
  8.3 0.5 multiply_power_fusion
  8.8 1.9 convert_reduce_fusion
  10.7 0.5 fusion.57
  11.2 0.1 copy-done.29
  11.3 0.6 copy-done.31
  11.9 4.2 convolution_add_fusion
  16.1 5.5 %copy.48 = f32[640,1536]{0,1:T(8,128)} copy(f32[640,1536]{1,0:T(8,128)} %convolution_add_fusion) | data formatting | bytes 7864320 | tf_op jit(solution)/shard_map/add | solution.py:102
  21.5 1.9 fusion.100
  23.5 0.2 copy_bitcast_fusion
  23.7 0.1 slice.150
  23.8 0.3 copy-done.40
  24.1 0.8 broadcast_multiply_fusion
  24.9 0.1 slice.151
  25.0 0.1 subtract_convert_fusion.1
  25.0 0.4 copy-done.22
  25.5 6.5 %fusion.4 = (f32[8,640]{1,0:T(8,128)S(1)}, f32[8,640,640]{1,2,0:T(8,128)}) fusion(pred[640,640]{0,1:T(8,128)(4,1)S(1)} %iota_compare_fusion, bf16[640,8,48]{0,2,1:T(8,128)(2,1)S(1)} %slice.150, bf16[640,8,8]{0,2,1:T(8,128)(2,1)S(1)} %get-tuple-element.49, bf16[640,8,8]{0,2,1:T(8,128)(2,1)S(1)} %get-tuple-element.50, bf16[640,8,48]{0,2,1:T(8,128)(2,1)S(1)} %slice.151, ...), kind=kOutput, calls=%fused_computation.8 | convolution fusion | flops 433187840 | bytes 14848000 | tf_op jit(solution)/shard_map/qhd,khd->hqk/dot_general | solution.py:70
  32.1 7.5 %exponential_reduce_fusion = f32[8,640]{1,0:T(8,128)S(1)} fusion(f32[8,640,640]{1,2,0:T(8,128)} %get-tuple-element.62, f32[8,640]{1,0:T(8,128)S(1)} %get-tuple-element.61, pred[640,640]{0,1:T(8,128)(4,1)S(1)} %iota_compare_fusion), kind=kLoop, calls=%fused_computation.6 | loop fusion | flops 13102080 | bytes 13557760 | tf_op jit(solution)/shard_map/reduce_sum | solution.py:110
  39.7 9.0 %convolution_convert_fusion.1 = bf16[8,64,640]{2,1,0:T(8,128)(2,1)} fusion(f32[8,640,640]{1,2,0:T(8,128)} %get-tuple-element.62, f32[8,640]{1,0:T(8,128)S(1)} %log_add_fusion, pred[640,640]{0,1:T(8,128)(4,1)S(1)} %iota_compare_fusion, f32[640,8,3,64]{0,3,2,1:T(8,128)S(1)} %bitcast.67), kind=kOutput, calls=%fused_computation.74 | convolution fusion | flops 432865280 | bytes 14848000 | tf_op jit(solution)/shard_map/hqk,khd->qhd/dot_general | solution.py:112
  48.7 1.0 convolution_convert_fusion
  49.7 9.1 %convolution_bitcast_fusion.2 = f32[640,8,1,64]{0,3,1,2:T(8,128)} fusion(bf16[640,8,64]{0,2,1:T(8,128)(2,1)S(1)} %bitcast.71, f32[8,640,640]{1,2,0:T(8,128)} %get-tuple-element.62, f32[8,640]{1,0:T(8,128)S(1)} %log_add_fusion, pred[640,640]{0,1:T(8,128)(4,1)S(1)} %iota_compare_fusion), kind=kOutput, calls=%fused_computation.72 | convolution fusion | flops 432537600 | bytes 15503360 | tf_op jit(solution)/shard_map/hqk,qhd->khd/dot_general | solution.py:133
  58.9 6.6 %fusion.74 = f32[8,640,640]{1,2,0:T(8,128)} fusion(bf16[640,8,64]{0,2,1:T(8,128)(2,1)S(1)} %bitcast.72, f32[640,8,3,64]{0,3,2,1:T(8,128)S(1)} %bitcast.68), kind=kOutput, calls=%fused_computation.91 | convolution fusion | flops 419430400 | bytes 14417920 | tf_op jit(solution)/shard_map/qhd,khd->hqk/dot_general | solution.py:136
  65.5 25.7 %fusion.65 = f32[640,8,64]{0,2,1:T(8,128)} fusion(f32[8,640,640]{1,2,0:T(8,128)} %fusion.74, f32[8,640,640]{1,2,0:T(8,128)} %get-tuple-element.62, f32[8,640]{1,0:T(8,128)} %copy-done.33, pred[640,640]{0,1:T(8,128)(4,1)S(1)} %iota_compare_fusion, bf16[640,8,48]{0,2,1:T(8,128)(2,1)} %copy-done.21, bf16[640,8,8]{0,2,1:T(8,128)(2,1)} %copy-done.27, ...), kind=kOutput, calls=%fused_computation.71 | convolution fusion | flops 457447040 | bytes 28610560 | tf_op jit(solution)/shard_map/hqk,qhd->khd/dot_general | solution.py:144
  91.2 25.7 %fusion.62 = f32[640,8,64]{0,2,1:T(8,128)} fusion(f32[8,640,640]{1,2,0:T(8,128)} %fusion.74, f32[8,640,640]{1,2,0:T(8,128)} %get-tuple-element.62, f32[8,640]{1,0:T(8,128)} %copy-done.33, pred[640,640]{0,1:T(8,128)(4,1)S(1)} %iota_compare_fusion, bf16[640,8,48]{0,2,1:T(8,128)(2,1)} %copy-done.20, bf16[640,8,8]{0,2,1:T(8,128)(2,1)} %copy-done.24, ...), kind=kOutput, calls=%fused_computation.70 | convolution fusion | flops 457447040 | bytes 28610560 | tf_op jit(solution)/shard_map/hqk,khd->qhd/dot_general | solution.py:141
  116.9 6.3 %multiply_convert_fusion.1 = (bf16[640,2048]{1,0:T(8,128)(2,1)S(1)}, f32[640,2048]{1,0:T(8,128)S(1)}) fusion(f32[2048]{0:T(1024)} %param.25, bf16[1024,2048]{1,0:T(8,128)(2,1)} %param.24, bf16[640,1024]{1,0:T(8,128)(2,1)} %param.14, f32[1024]{0:T(1024)} %param.19, f32[1024]{0:T(1024)} %param.18, f32[640]{0:T(1024)} %copy-done.31, f32[640]{0:T(1024)} %copy-done.29), kind=kOutput, calls=%fused_computation.26 | convolution fusion | flops 2696151040 | bytes 13390848 | tf_op jit(solution)/shard_map/dot_general | solution.py:114
  123.2 2.9 fusion.103
  126.2 5.4 %fusion.102 = (f32[2048]{0:T(1024)S(1)}, bf16[640,2048]{1,0:T(8,128)(2,1)S(1)}) fusion(f32[640,2048]{1,0:T(8,128)S(1)} %get-tuple-element.60, f32[2048]{0:T(1024)S(1)} %copy-done.44, bf16[640,1024]{1,0:T(8,128)(2,1)S(1)} %copy-done.15, bf16[2048,1024]{1,0:T(8,128)(2,1)S(1)} %copy-done.41), kind=kOutput, calls=%fused_computation.126 | convolution fusion | flops 2700081152 | bytes 13385728 | tf_op jit(solution)/shard_map/dot_general | solution.py:123
  131.6 4.5 %fusion.70 = f32[640,1024]{1,0:T(8,128)} fusion(bf16[1024,2048]{1,0:T(8,128)(2,1)S(1)} %copy-done.42, bf16[640,2048]{1,0:T(8,128)(2,1)S(1)} %get-tuple-element.64), kind=kOutput, calls=%fused_computation.82 | convolution fusion | flops 2684354560 | bytes 9437184 | tf_op jit(solution)/shard_map/dot_general | solution.py:128
  136.1 1.3 copy-done.11
  137.4 0.4 copy-done.12
  137.8 0.1 multiply_subtract_fusion.1
  137.9 0.3 slice-done.1
  138.2 0.1 maximum_bitcast_fusion.1
  138.3 0.2 slice-done
  138.5 0.1 maximum_bitcast_fusion
  138.6 1.5 copy-done.10
  140.0 0.4 fusion.44
  140.5 0.7 copy-done.6
  141.1 0.2 copy.56
  141.3 3.7 fusion.104
  145.1 2.4 convolution_add_fusion.1
  147.5 0.0 all-reduce.4.cloned.1.call-update
  147.6 0.0 reduce-scatter.2.cloned.1.call-start
  147.6 3.9 convolution_bitcast_fusion.1
  151.5 3.2 copy.58
  154.8 6.0 %fusion.97 = f32[1024,1536]{1,0:T(8,128)S(1)} fusion(bf16[640,1536]{0,1:T(8,128)(2,1)} %bitcast.70, bf16[640,1024]{1,0:T(8,128)(2,1)} %param.14, f32[1024]{0:T(1024)S(1)} %copy-done.46, f32[1024]{0:T(1024)S(1)} %copy-done.36, f32[640]{0:T(1024)S(1)} %copy-done.32, f32[640]{0:T(1024)S(1)} %copy-done.30), kind=kOutput, calls=%fused_computation.123 | convolution fusion | flops 2017198080 | bytes 9581568 | tf_op jit(solution)/shard_map/dot_general | solution.py:63
  160.9 3.6 convolution_bitcast_fusion
  164.6 3.7 fusion.68
  168.3 8.9 %pad_maximum_fusion = f32[1024,6144]{1,0:T(8,128)} fusion(f32[1024,2048]{1,0:T(8,128)S(1)} %convolution_bitcast_fusion, f32[1024,2048]{1,0:T(8,128)S(1)} %fusion.68, f32[1024,512]{1,0:T(8,128)S(1)} %copy-done.9, f32[1024,1536]{1,0:T(8,128)S(1)} %fusion.97), kind=kLoop, calls=%fused_computation.1 | loop fusion | flops 18874368 | bytes 50331648 | tf_op jit(solution)/shard_map/concatenate | solution.py:152
  177.2 0.0 reduce-scatter.2.cloned.1.call-update
  177.2 2.4 fusion.43
  179.6 0.1 reduce_sum.151
  179.7 158.0 %all-reduce.4.cloned.1.call-done = (f32[640,1024]{1,0:T(8,128)}, f32[640,1024]{1,0:T(8,128)}, f32[640,1024]{1,0:T(8,128)}) async-done(((f32[640,1024]{1,0:T(8,128)}, f32[640,1024]{1,0:T(8,128)}, f32[640,1024]{1,0:T(8,128)}), (f32[640,1024]{1,0:T(8,128)}, f32[640,1024]{1,0:T(8,128)}, f32[640,1024]{1,0:T(8,128)})) %all-reduce.4.cloned.1.call-update) | async-done | bytes 7864336 | tf_op jit(solution)/shard_map/psum | solution.py:119
  337.7 4.9 %fusion.55 = (f32[1024]{0:T(1024)S(1)}, f32[640]{0:T(1024)S(1)}, f32[640]{0:T(1024)S(1)}, f32[1024]{0:T(1024)S(1)}, f32[1024]{0:T(1024)S(1)}, /*index=5*/f32[640]{0:T(1024)S(1)}, f32[640]{0:T(1024)S(1)}, f32[1024]{0:T(1024)S(1)}) fusion(f32[640,1024]{1,0:T(8,128)} %get-tuple-element.31, bf16[640,1024]{1,0:T(8,128)(2,1)} %param.14, f32[640]{0:T(1024)S(1)} %copy-done.32, ...), kind=kLoop, calls=%fused_computation.58 | loop fusion | flops 11134464 | bytes 6593536 | tf_op jit(solution)/shard_map/reduce_sum | solution.py:175
  342.7 0.5 copy-done.8
  343.2 4.7 %convert_reduce_fusion.1 = (f32[1024]{0:T(1024)S(1)}, bf16[640,1024]{1,0:T(8,128)(2,1)}, bf16[640,1024]{1,0:T(8,128)(2,1)}) fusion(bf16[640,1024]{1,0:T(8,128)(2,1)} %param.15, f32[640]{0:T(1024)S(1)} %broadcast_multiply_fusion.1, f32[640]{0:T(1024)S(1)} %broadcast_multiply_fusion.2, f32[640,1024]{1,0:T(8,128)S(1)} %copy-done.7, f32[1024]{0:T(1024)S(1)} %copy-done.34, ...), kind=kLoop, calls=%fused_computation.34 | loop fusion | flops 13761536 | bytes 13143040 | tf_op jit(solution)/shard_map/reduce_sum | solution.py:122
  347.9 64.7 %all-reduce = (f32[5,1024]{1,0:T(8,128)S(1)}, f32[1536]{0:T(1024)}, f32[2048]{0:T(1024)}) all-reduce(f32[5,1024]{1,0:T(8,128)S(1)} %stack.39, f32[1536]{0:T(1024)S(1)} %reduce_sum.151, f32[2048]{0:T(1024)S(1)} %get-tuple-element.63), channel_id=1, replica_groups=mesh['dp'=16,'tensor'=2] {'dp'}, use_global_device_ids=true, to_apply=%region_17.18 | all-reduce | flops 8704 | bytes 69632 | tf_op jit(solution)/shard_map/psum | solution.py:186
  412.6 0.6 fusion.101
  413.2 10.0 %reduce-scatter.2.cloned.1.call-done = f32[64,6144]{1,0:T(8,128)} async-done(((f32[1024,6144]{1,0:T(8,128)}), f32[64,6144]{1,0:T(8,128)}) %reduce-scatter.2.cloned.1.call-update) | async-done | bytes 1572880 | tf_op jit(solution)/shard_map/reduce_scatter | solution.py:151
  423.2 1.8 slice.125
  425.0 1.6 slice_bitcast_fusion.1
  426.6 2.3 slice_bitcast_fusion
  428.8 0.6 copy.79
  (106 shorter events, 0.3 us)
Async XLA Ops:
  8.0 3.9 copy-start
  8.0 329.7 %all-reduce.4.cloned.1.call-start = ((), (), s32[]{:S(2)}) async-start(), calls=%async_computation.2 | async-start | bytes 15728640 | tf_op jit(solution)/shard_map/psum | solution.py:119
  8.1 2.6 copy-start.1
  8.1 3.8 copy-start.35
  8.1 3.8 copy-start.43
  8.1 3.8 copy-start.45
  10.7 0.6 copy-start.29
  11.3 0.6 copy-start.31
  23.5 0.7 copy-start.40
  24.1 7.9 %copy-start.20 = (bf16[640,8,48]{0,2,1:T(8,128)(2,1)}, bf16[640,8,48]{0,2,1:T(8,128)(2,1)S(1)}, u32[]{:S(2)}) copy-start(bf16[640,8,48]{0,2,1:T(8,128)(2,1)S(1)} %slice.150) | copy-start | bytes 1474564
  24.9 0.6 copy-start.22
  24.9 7.1 %copy-start.21 = (bf16[640,8,48]{0,2,1:T(8,128)(2,1)}, bf16[640,8,48]{0,2,1:T(8,128)(2,1)S(1)}, u32[]{:S(2)}) copy-start(bf16[640,8,48]{0,2,1:T(8,128)(2,1)S(1)} %slice.151) | copy-start | bytes 1474564
  25.5 6.5 %copy-start.24 = (bf16[640,8,8]{0,2,1:T(8,128)(2,1)}, bf16[640,8,8]{0,2,1:T(8,128)(2,1)S(1)}, u32[]{:S(2)}) copy-start(bf16[640,8,8]{0,2,1:T(8,128)(2,1)S(1)} %get-tuple-element.49) | copy-start | bytes 245764
  25.5 6.6 %copy-start.25 = (bf16[640,8,8]{0,2,1:T(8,128)(2,1)}, bf16[640,8,8]{0,2,1:T(8,128)(2,1)S(1)}, u32[]{:S(2)}) copy-start(bf16[640,8,8]{0,2,1:T(8,128)(2,1)S(1)} %get-tuple-element.50) | copy-start | bytes 245764
  25.5 6.6 %copy-start.26 = (bf16[640,8,8]{0,2,1:T(8,128)(2,1)}, bf16[640,8,8]{0,2,1:T(8,128)(2,1)S(1)}, u32[]{:S(2)}) copy-start(bf16[640,8,8]{0,2,1:T(8,128)(2,1)S(1)} %get-tuple-element.40) | copy-start | bytes 245764
  25.5 6.6 %copy-start.27 = (bf16[640,8,8]{0,2,1:T(8,128)(2,1)}, bf16[640,8,8]{0,2,1:T(8,128)(2,1)S(1)}, u32[]{:S(2)}) copy-start(bf16[640,8,8]{0,2,1:T(8,128)(2,1)S(1)} %get-tuple-element.41) | copy-start | bytes 245764
  32.1 7.6 %copy-start.4 = (f32[640,1536]{0,1:T(8,128)S(1)}, f32[640,1536]{0,1:T(8,128)}, u32[]{:S(2)}) copy-start(f32[640,1536]{0,1:T(8,128)} %copy.48) | copy-start | bytes 11796484
  39.6 10.1 %copy-start.33 = (f32[8,640]{1,0:T(8,128)}, f32[8,640]{1,0:T(8,128)S(1)}, u32[]{:S(2)}) copy-start(f32[8,640]{1,0:T(8,128)S(1)} %log_add_fusion) | copy-start | bytes 61444
  39.7 9.1 %copy-start.14 = (bf16[640,1024]{1,0:T(8,128)(2,1)S(1)}, bf16[640,1024]{1,0:T(8,128)(2,1)}, u32[]{:S(2)}) copy-start(bf16[640,1024]{1,0:T(8,128)(2,1)} %param.15) | copy-start | bytes 3932164
  39.7 9.0 %copy-start.17 = (bf16[512,1024]{1,0:T(8,128)(2,1)S(1)}, bf16[512,1024]{1,0:T(8,128)(2,1)}, u32[]{:S(2)}) copy-start(bf16[512,1024]{1,0:T(8,128)(2,1)} %param.22) | copy-start | bytes 3145732
  116.9 6.3 %copy-start.41 = (bf16[2048,1024]{1,0:T(8,128)(2,1)S(1)}, bf16[2048,1024]{1,0:T(8,128)(2,1)}, u32[]{:S(2)}) copy-start(bf16[2048,1024]{1,0:T(8,128)(2,1)} %param.26) | copy-start | bytes 12582916
  123.2 2.9 copy-start.48
  123.2 2.9 copy-start.15
  123.2 2.9 copy-start.44
  126.1 5.4 %copy-start.42 = (bf16[1024,2048]{1,0:T(8,128)(2,1)S(1)}, bf16[1024,2048]{1,0:T(8,128)(2,1)}, u32[]{:S(2)}) copy-start(bf16[1024,2048]{1,0:T(8,128)(2,1)} %param.24) | copy-start | bytes 12582916
  131.6 4.5 %copy-start.50 = (bf16[640,2048]{1,0:T(8,128)(2,1)}, bf16[640,2048]{1,0:T(8,128)(2,1)S(1)}, u32[]{:S(2)}) copy-start(bf16[640,2048]{1,0:T(8,128)(2,1)S(1)} %get-tuple-element.64) | copy-start | bytes 7864324
  136.1 1.3 copy-start.11
  136.1 1.7 copy-start.12
  136.1 1.7 copy-start.23
  136.1 1.7 copy-start.28
  136.1 2.1 slice-start.1
  136.1 2.4 slice-start
  138.2 1.9 copy-start.10
  138.3 2.2 copy-start.5
  140.0 1.1 copy-start.6
  141.3 3.8 copy-start.13
  141.3 3.8 copy-start.18
  141.3 3.8 copy-start.19
  147.6 275.7 %reduce-scatter.2.cloned.1.call-start = ((), (), s32[]{:S(2)}) async-start(), calls=%async_computation.1 | async-start | bytes 26738688 | tf_op jit(solution)/shard_map/reduce_scatter | solution.py:151
  151.5 3.2 copy-start.30
  151.5 3.2 copy-start.32
  151.5 3.2 copy-start.36
  151.5 3.2 copy-start.46
  154.8 6.1 %copy-start.16 = (bf16[640,1024]{1,0:T(8,128)(2,1)S(1)}, bf16[640,1024]{1,0:T(8,128)(2,1)}, u32[]{:S(2)}) copy-start(bf16[640,1024]{1,0:T(8,128)(2,1)} %param.15) | copy-start | bytes 3932164
  154.8 6.1 %copy-start.49 = (bf16[640,2048]{1,0:T(8,128)(2,1)S(1)}, bf16[640,2048]{1,0:T(8,128)(2,1)}, u32[]{:S(2)}) copy-start(bf16[640,2048]{1,0:T(8,128)(2,1)} %copy-done.48) | copy-start | bytes 7864324
  160.9 3.7 copy-start.2
  160.9 3.7 copy-start.34
  160.9 3.7 copy-start.47
  160.9 3.7 copy-start.51
  164.6 3.8 copy-start.9
  337.7 5.0 %copy-start.3 = (bf16[640,1024]{1,0:T(8,128)(2,1)S(1)}, bf16[640,1024]{1,0:T(8,128)(2,1)}, u32[]{:S(2)}) copy-start(bf16[640,1024]{1,0:T(8,128)(2,1)} %param.14) | copy-start | bytes 3932164
  337.7 5.0 %copy-start.7 = (f32[640,1024]{1,0:T(8,128)S(1)}, f32[640,1024]{1,0:T(8,128)}, u32[]{:S(2)}) copy-start(f32[640,1024]{1,0:T(8,128)} %get-tuple-element.30) | copy-start | bytes 7864324
  337.7 5.4 %copy-start.8 = (f32[640,1024]{1,0:T(8,128)S(1)}, f32[640,1024]{1,0:T(8,128)}, u32[]{:S(2)}) copy-start(f32[640,1024]{1,0:T(8,128)} %get-tuple-element.31) | copy-start | bytes 7864324
  337.7 5.4 %copy-start.38 = (f32[1024]{0:T(1024)S(1)}, f32[1024]{0:T(1024)}, u32[]{:S(2)}) copy-start(f32[1024]{0:T(1024)} %param.27) | copy-start | bytes 12292
  337.7 5.4 %copy-start.39 = (f32[1024]{0:T(1024)S(1)}, f32[1024]{0:T(1024)}, u32[]{:S(2)}) copy-start(f32[1024]{0:T(1024)} %param.23) | copy-start | bytes 12292
  413.2 16.2 %copy-start.37 = (f32[1,1024]{1,0:T(1,128)}, f32[1,1024]{1,0:T(1,128)S(1)}, u32[]{:S(2)}) copy-start(f32[1,1024]{1,0:T(1,128)S(1)} %get-tuple-element.51) | copy-start | bytes 12292
Sparse Core Ops, SparseCore 0:
  147.7 189.9 all-reduce.3
Sparse Core Ops, SparseCore 1:
  177.3 245.9 reduce-scatter.1
where the time goes:
time: 442 us; the launch traced here: 437 us
  waiting for transfers between devices  168 us (38%)
  matrix products  130 us (29%)
  blocking collectives  64.7 us (15%)
  other arithmetic  33 us (7%)
  local copies, waits for them, and re-layouts  24.5 us (6%)
  between operations  16.8 us (4%)
    psum x1, waiting for transfers between devices, body(): branches = lax.psum(partial_out, 'tensor')  158 us
    psum x1, blocking collectives, body(): lax.psum((vectors, qkv_bias_term, expand_bias_term), 'dp')  64.7 us
    dot_general x1, matrix products, body(): jnp.einsum('hqk,qhd->khd', score_grad, queries, preferred_element_type=jn...  25.7 us
    dot_general x1, matrix products, body(): jnp.einsum('hqk,khd->qhd', score_grad, keys_rot, preferred_element_type=j...  25.7 us
    dot_general x4, matrix products, column_products(): lax.dot_general(left_cols, right_rows, (((0,), (0,)), ((), ())), preferre...  17.3 us
    reduce_scatter x1, waiting for transfers between devices, body(): lax.psum_scatter(jnp.concatenate([jnp.concatenate([column_products(ln_att...  9.99 us
    dot_general x1, matrix products, body(): jnp.einsum('hqk,qhd->khd', probs_again, context_grad, preferred_element_t...  9.11 us
    dot_general x1, matrix products, body(): jnp.einsum('hqk,khd->qhd', probs_low, values_low, preferred_element_type=...  9.03 us
  transfers between devices with their start and end apart: 2, of which 2 were waited for; matrix products, arithmetic and copies ran while one was open for 10% of the time, Pallas kernels for 0%

commit v1 on v0

v1 whole, which is shorter than its diff:
```python
import functools

import jax
import jax.numpy as jnp
from jax import lax
from jax.experimental import pallas as pl
from jax.experimental.pallas import tpu as pltpu
from jax.sharding import PartitionSpec as P

HEAD_DIM = 64
ROT = 16


NORM_EPS = 1e-05
SQRT_HALF = 0.7071067811865476
INV_ROOT_TWO_PI = 0.3989422804014327


def normalize(values):
    center = values - jnp.mean(values, axis=1, keepdims=True)
    inverse = lax.rsqrt(jnp.mean(center * center, axis=1, keepdims=True) + NORM_EPS)
    return (center * inverse, inverse)


def rotary_tables(length):
    halfway = ROT // 2
    frequency = 10000.0 ** (-2.0 * jnp.arange(halfway, dtype=jnp.float32) / ROT)
    angles = jnp.arange(length, dtype=jnp.float32)[:, None] * frequency[None, :]
    cosine, sine = jnp.cos(angles), jnp.sin(angles)
    zeros = jnp.zeros((length, halfway), jnp.float32)
    rest_ones = jnp.ones((length, HEAD_DIM - ROT), jnp.float32)
    rest_zeros = jnp.zeros((length, HEAD_DIM - ROT), jnp.float32)
    whole = jnp.ones((length, HEAD_DIM), jnp.float32)
    blank = jnp.zeros((length, HEAD_DIM), jnp.float32)
    keep = jnp.concatenate([cosine, cosine, rest_ones], axis=1)
    ahead = jnp.concatenate([-sine, zeros, rest_zeros], axis=1)
    behind = jnp.concatenate([zeros, sine, rest_zeros], axis=1)
    return (
        jnp.concatenate([keep, keep, whole] * 2, axis=1),
        jnp.concatenate([ahead, ahead, blank] * 2, axis=1),
        jnp.concatenate([behind, behind, blank] * 2, axis=1),
    )


def gelu_value(hidden_in):
    return 0.5 * hidden_in * (1.0 + lax.erf(hidden_in * SQRT_HALF))


def gelu_slope(hidden_in):
    return (
        0.5 * (1.0 + lax.erf(hidden_in * SQRT_HALF))
        + hidden_in * jnp.exp(-0.5 * hidden_in * hidden_in) * INV_ROOT_TWO_PI
    )


def column_products(left_cols, right_rows):
    return lax.dot_general(
        left_cols, right_rows, (((0,), (0,)), ((), ())), preferred_element_type=jnp.float32
    )


NT = (((1,), (1,)), ((), ()))
TN = (((0,), (0,)), ((), ()))
PAIR = 6 * HEAD_DIM
LANES = 128


def dot32(left, right, dims=(((1,), (0,)), ((), ()))):
    return lax.dot_general(left, right, dims, preferred_element_type=jnp.float32)


def attention_kernel(
    ln_ref,
    up_ref,
    weight_ref,
    bias_ref,
    dense_ref,
    keep_ref,
    ahead_ref,
    behind_ref,
    context_ref,
    mixed_low_ref,
    bias_grad_ref,
    qkv_s,
    context_grad_s,
    grad_s,
):
    length = ln_ref.shape[0]
    block = LANES if length % LANES == 0 else length
    scale = HEAD_DIM ** (-0.5)
    mixed = dot32(ln_ref[...], weight_ref[...]) + bias_ref[...]
    for tile in range(PAIR // LANES):
        lanes = slice(tile * LANES, (tile + 1) * LANES)
        x = mixed[:, lanes]
        turned = (
            x * keep_ref[:, lanes]
            + pltpu.roll(x, LANES - ROT // 2, 1) * ahead_ref[:, lanes]
            + pltpu.roll(x, ROT // 2, 1) * behind_ref[:, lanes]
        )
        qkv_s[:, lanes] = turned.astype(jnp.bfloat16)
    context_grad_s[...] = dot32(up_ref[...], dense_ref[...], NT).astype(jnp.bfloat16)
    grad_s[...] = jnp.zeros_like(grad_s)
    for head in range(2):
        at = 3 * HEAD_DIM * head
        q_cols = slice(at, at + HEAD_DIM)
        k_cols = slice(at + HEAD_DIM, at + 2 * HEAD_DIM)
        v_cols = slice(at + 2 * HEAD_DIM, at + 3 * HEAD_DIM)
        own = slice(head * HEAD_DIM, (head + 1) * HEAD_DIM)
        for first in range(0, length, block):
            end = first + block
            rows = slice(first, end)
            q = qkv_s[rows, q_cols]
            k = qkv_s[:end, k_cols]
            v = qkv_s[:end, v_cols]
            context_grad = context_grad_s[rows, own]
            scores = dot32(q, k, NT) * scale
            row = lax.broadcasted_iota(jnp.int32, (block, end), 0) + first
            col = lax.broadcasted_iota(jnp.int32, (block, end), 1)
            scores = jnp.where(row >= col, scores, -jnp.inf)
            powers = jnp.exp(scores - jnp.max(scores, axis=1, keepdims=True))
            probs = powers * (1.0 / jnp.sum(powers, axis=1, keepdims=True))
            probs_low = probs.astype(jnp.bfloat16)
            context_ref[rows, own] = dot32(probs_low, v).astype(jnp.bfloat16)
            prob_grad = dot32(context_grad, v, NT)
            delta = jnp.sum(probs * prob_grad, axis=1, keepdims=True)
            score_grad = (probs * (prob_grad - delta) * scale).astype(jnp.bfloat16)
            grad_s[rows, q_cols] = dot32(score_grad, k)
            grad_s[:end, k_cols] += dot32(score_grad, q, TN)
            grad_s[:end, v_cols] += dot32(probs_low, context_grad, TN)
    for tile in range(PAIR // LANES):
        lanes = slice(tile * LANES, (tile + 1) * LANES)
        x = grad_s[:, lanes]
        back = (
            x * keep_ref[:, lanes]
            - pltpu.roll(x, LANES - ROT // 2, 1) * ahead_ref[:, lanes]
            - pltpu.roll(x, ROT // 2, 1) * behind_ref[:, lanes]
        )
        bias_grad_ref[:, lanes] = jnp.sum(back, axis=0, keepdims=True)
        mixed_low_ref[:, lanes] = back.astype(jnp.bfloat16)


def attention(ln_attn, upstream, qkv_weight, qkv_bias, dense_weight):
    length, width = ln_attn.shape
    qkv_cols = qkv_weight.shape[1]
    pairs = qkv_cols // PAIR
    tables = rotary_tables(length)
    whole = lambda p: (0, 0)
    across = lambda p: (0, p)
    return pl.pallas_call(
        attention_kernel,
        grid=(pairs,),
        in_specs=[
            pl.BlockSpec((length, width), whole),
            pl.BlockSpec((length, width), whole),
            pl.BlockSpec((width, PAIR), across),
            pl.BlockSpec((1, PAIR), across),
            pl.BlockSpec((2 * HEAD_DIM, width), lambda p: (p, 0)),
            pl.BlockSpec((length, PAIR), whole),
            pl.BlockSpec((length, PAIR), whole),
            pl.BlockSpec((length, PAIR), whole),
        ],
        out_specs=[
            pl.BlockSpec((length, 2 * HEAD_DIM), across),
            pl.BlockSpec((length, PAIR), across),
            pl.BlockSpec((1, PAIR), across),
        ],
        out_shape=[
            jax.ShapeDtypeStruct((length, pairs * 2 * HEAD_DIM), jnp.bfloat16),
            jax.ShapeDtypeStruct((length, qkv_cols), jnp.bfloat16),
            jax.ShapeDtypeStruct((1, qkv_cols), jnp.float32),
        ],
        scratch_shapes=[
            pltpu.VMEM((length, PAIR), jnp.bfloat16),
            pltpu.VMEM((length, 2 * HEAD_DIM), jnp.bfloat16),
            pltpu.VMEM((length, PAIR), jnp.float32),
        ],
        compiler_params=pltpu.CompilerParams(vmem_limit_bytes=40 * 1024 * 1024),
        cost_estimate=pl.CostEstimate(
            flops=2 * length * width * qkv_cols * 6,
            bytes_accessed=16 * 1024 * 1024,
            transcendentals=0,
        ),
    )(ln_attn, upstream, qkv_weight, qkv_bias.reshape(1, qkv_cols), dense_weight, *tables)


def tensor_sum(part, shards):
    if shards == 2:
        return part + lax.ppermute(part, "tensor", [(0, 1), (1, 0)])
    return lax.psum(part, "tensor")


def scatter_sum(term):
    return lax.psum_scatter(term, "dp", scatter_dimension=0, tiled=True)


def body(
    shards,
    layer_input,
    output_grad,
    attn_gain,
    attn_shift,
    mlp_gain,
    mlp_shift,
    qkv_weight,
    qkv_bias,
    dense_weight,
    dense_bias,
    expand_weight,
    expand_bias,
    contract_weight,
    contract_bias,
):
    qkv_cols = qkv_weight.shape[1]
    ff_here = expand_weight.shape[1]
    width = layer_input.shape[1]
    wide_input = layer_input.astype(jnp.float32)
    unit_rows, inverse = normalize(wide_input)
    ln_attn = (unit_rows * attn_gain + attn_shift).astype(jnp.bfloat16)
    ln_mlp = (unit_rows * mlp_gain + mlp_shift).astype(jnp.bfloat16)
    context, mixed_low, qkv_bias_term = attention(
        ln_attn, output_grad, qkv_weight, qkv_bias, dense_weight
    )
    hidden = dot32(ln_mlp, expand_weight) + expand_bias
    active = gelu_value(hidden).astype(jnp.bfloat16)
    partial_out = dot32(context, dense_weight) + dot32(active, contract_weight)
    branches = tensor_sum(partial_out, shards)
    layer_output = (wide_input + branches + dense_bias + contract_bias).astype(jnp.bfloat16)
    upstream_f = output_grad.astype(jnp.float32)
    active, hidden, mixed_low, _ = lax.optimization_barrier(
        (active, hidden, mixed_low, partial_out)
    )
    contract_summed = scatter_sum(column_products(output_grad, active))
    hidden_grad = dot32(output_grad, contract_weight, NT) * gelu_slope(hidden)
    expand_bias_term = jnp.sum(hidden_grad, axis=0)
    hidden_low = hidden_grad.astype(jnp.bfloat16)
    mlp_norm_part = dot32(hidden_low, expand_weight, NT)
    attn_norm_part = dot32(mixed_low, qkv_weight, NT)
    scaled_part = attn_norm_part * attn_gain + mlp_norm_part * mlp_gain
    scaled = tensor_sum(scaled_part, shards)
    hidden_low, mixed_low, context, _ = lax.optimization_barrier(
        (hidden_low, mixed_low, context, scaled_part)
    )
    expand_summed = scatter_sum(column_products(ln_mlp, hidden_low))
    qkv_summed = scatter_sum(column_products(ln_attn, mixed_low))
    dense_summed = scatter_sum(column_products(output_grad, context))
    me = lax.axis_index("tensor")
    slots = jnp.arange(shards)[:, None] == me
    small = jnp.concatenate(
        [
            jnp.sum(attn_norm_part * unit_rows, axis=0),
            jnp.sum(attn_norm_part, axis=0),
            jnp.sum(mlp_norm_part * unit_rows, axis=0),
            jnp.sum(mlp_norm_part, axis=0),
            jnp.where(me == 0, jnp.sum(upstream_f, axis=0), 0.0),
            jnp.where(slots, qkv_bias_term, 0.0).reshape(-1),
            jnp.where(slots, expand_bias_term[None], 0.0).reshape(-1),
        ]
    )
    small = lax.psum(small, ("dp", "tensor"))
    vectors = small[: 5 * width].reshape(5, width)
    qkv_bias_grad = lax.dynamic_slice(small, (5 * width + me * qkv_cols,), (qkv_cols,))
    expand_bias_grad = lax.dynamic_slice(
        small, (5 * width + shards * qkv_cols + me * ff_here,), (ff_here,)
    )
    input_back = inverse * (
        scaled
        - jnp.mean(scaled, axis=1, keepdims=True)
        - unit_rows * jnp.mean(scaled * unit_rows, axis=1, keepdims=True)
    )
    input_grad = (upstream_f + input_back).astype(jnp.bfloat16)
    return (
        layer_output,
        input_grad,
        vectors[0],
        vectors[1],
        vectors[2],
        vectors[3],
        qkv_summed,
        qkv_bias_grad,
        dense_summed.T,
        vectors[4],
        expand_summed,
        expand_bias_grad,
        contract_summed.T,
        vectors[4],
    )


def solution(mesh):
    in_specs = (
        P("dp", None),
        P("dp", None),
        P(),
        P(),
        P(),
        P(),
        P(None, "tensor"),
        P("tensor"),
        P("tensor", None),
        P(),
        P(None, "tensor"),
        P("tensor"),
        P("tensor", None),
        P(),
    )
    out_specs = (
        P("dp", None),
        P("dp", None),
        P(),
        P(),
        P(),
        P(),
        P("dp", "tensor"),
        P("tensor"),
        P("tensor", "dp"),
        P(),
        P("dp", "tensor"),
        P("tensor"),
        P("tensor", "dp"),
        P(),
    )
    return jax.shard_map(
        functools.partial(body, mesh.shape["tensor"]),
        mesh=mesh,
        in_specs=in_specs,
        out_specs=out_specs,
        check_vma=False,
    )
```

time: 442 us -> 487 us (1.10)
  waiting for transfers between devices: 168 us -> 281 us
  matrix products: 130 us -> 52.3 us
  Pallas kernels: 0 us -> 38.6 us
  blocking collectives: 64.7 us -> 41.5 us
  other arithmetic: 33 us -> 12.9 us
  local copies, waits for them, and re-layouts: 24.5 us -> 41.8 us
    psum x1 -> x0, waiting for transfers between devices: 158 us -> none  [body(): branches = lax.psum(partial_out, 'tensor')]
    ppermute x0 -> x2, waiting for transfers between devices: none -> 109 us  [tensor_sum(): return part + lax.ppermute(part, 'tensor', [(0, 1), (1, 0)])]
    unnamed x2 -> x6, waiting for transfers between devices: 0.03 us -> 108 us
    dot_general x14 -> x6, matrix products: 113 us -> 28.3 us  [dot32(): lax.dot_general(left, right, dims, preferred_element_type=jnp.float32)]
    reduce_scatter x1 -> x2, waiting for transfers between devices: 9.99 us -> 64.2 us  [scatter_sum(): return lax.psum_scatter(term, 'dp', scatter_dimension=0, tiled=True)]
    pallas_call x0 -> x1, Pallas kernels: none -> 38.6 us  [attention(): pl.pallas_call(attention_kernel, grid=(pairs,), in_specs=[pl.BlockSpec((l...]
    psum x1, blocking collectives: 64.7 us -> 41.5 us  [body(): small = lax.psum(small, ('dp', 'tensor'))]
    unnamed x105 -> x61, local copies, waits for them, and re-layouts: 6.52 us -> 23.8 us
  transfers between devices with their start and end apart: 2 -> 6, of which waited for: 2 -> 4; matrix products, arithmetic and copies ran while one was open for 10% -> 8% of each run, Pallas kernels for 0% -> 0%
where the time goes in v1:
time: 487 us; the launch traced here: 486 us
  waiting for transfers between devices  281 us (58%)
  matrix products  52.3 us (11%)
  local copies, waits for them, and re-layouts  41.8 us (9%)
  blocking collectives  41.5 us (9%)
  Pallas kernels  38.6 us (8%)
  between operations  14.1 us (3%)
  other arithmetic  12.9 us (3%)
    ppermute x2, waiting for transfers between devices, tensor_sum(): return part + lax.ppermute(part, 'tensor', [(0, 1), (1, 0)])  109 us
    unnamed x6, waiting for transfers between devices  108 us
    reduce_scatter x2, waiting for transfers between devices, scatter_sum(): return lax.psum_scatter(term, 'dp', scatter_dimension=0, tiled=True)  64.2 us
    psum x1, blocking collectives, body(): small = lax.psum(small, ('dp', 'tensor'))  41.5 us
    pallas_call x1, Pallas kernels, attention(): pl.pallas_call(attention_kernel, grid=(pairs,), in_specs=[pl.BlockSpec((l...  38.6 us
    dot_general x6, matrix products, dot32(): lax.dot_general(left, right, dims, preferred_element_type=jnp.float32)  28.3 us
    dot_general x4, matrix products, column_products(): lax.dot_general(left_cols, right_rows, (((0,), (0,)), ((), ())), preferre...  24.1 us
    unnamed x61, local copies, waits for them, and re-layouts  23.8 us
  transfers between devices with their start and end apart: 6, of which 4 were waited for; matrix products, arithmetic and copies ran while one was open for 8% of the time, Pallas kernels for 0%

profile of v1, /device:TPU:0, one launch (start us, length us, event | category | flops | bytes accessed | tf_op | source)
XLA Modules:
  0.0 485.7 jit_solution(14829458314209758234)
XLA Ops:
  7.2 0.0 reduce-scatter.13.cloned.1.call-start
  7.2 1.6 convert_reduce_fusion
  8.8 1.8 fusion.22
  10.6 1.2 fusion.27
  12.0 4.9 %concatenate.20.behind_ref = f32[640,384]{1,0:T(8,128)} concatenate(f32[640,8]{1,0:T(8,128)S(1)} %broadcast_in_dim.80, f32[640,8]{1,0:T(8,128)S(1)} %get-tuple-element.80, f32[640,48]{1,0:T(8,128)S(1)} %broadcast_in_dim.81, f32[640,8]{1,0:T(8,128)S(1)} %broadcast_in_dim.80, f32[640,8]{1,0:T(8,128)S(1)} %get-tuple-element.80, f32[640,48]{1,0:T(8,128)S(1)} %broadcast_in_dim.81, ...), dimensions={1} | concatenate | bytes 1966080 | tf_op jit(solution)/shard_map/concatenate | solution.py:41
  16.8 4.9 %concatenate.19.ahead_ref = f32[640,384]{1,0:T(8,128)} concatenate(f32[640,8]{1,0:T(8,128)S(1)} %get-tuple-element.81, f32[640,8]{1,0:T(8,128)S(1)} %broadcast_in_dim.80, f32[640,48]{1,0:T(8,128)S(1)} %broadcast_in_dim.81, f32[640,8]{1,0:T(8,128)S(1)} %get-tuple-element.81, f32[640,8]{1,0:T(8,128)S(1)} %broadcast_in_dim.80, f32[640,48]{1,0:T(8,128)S(1)} %broadcast_in_dim.81, ...), dimensions={1} | concatenate | bytes 1966080 | tf_op jit(solution)/shard_map/concatenate | solution.py:40
  21.7 0.0 copy-start.21
  21.7 0.0 copy-start.22
  21.7 0.0 copy-start.23
  21.8 0.5 fusion.14.ln_ref
  22.3 0.1 copy-done.21
  22.4 0.0 copy-done.22
  22.4 0.0 copy-done.23
  22.4 7.7 %multiply_convert_fusion = (bf16[640,2048]{1,0:T(8,128)(2,1)S(1)}, f32[640,2048]{1,0:T(8,128)}) fusion(f32[2048]{0:T(1024)S(1)} %copy-done.21, bf16[1024,2048]{1,0:T(8,128)(2,1)} %param.24, bf16[640,1024]{1,0:T(8,128)(2,1)S(1)} %copy-done.7, f32[1024]{0:T(1024)S(1)} %copy-done.23, f32[1024]{0:T(1024)S(1)} %copy-done.22, f32[640]{0:T(1024)S(1)} %add_rsqrt_fusion, ...), kind=kOutput, calls=%fused_computation.6 | convolution fusion | flops 2696151040 | bytes 13390848 | tf_op jit(solution)/shard_map/dot_general | solution.py:69
  30.2 4.4 fusion.38
  34.6 0.7 broadcast_in_dim.79
  35.4 0.0 copy-start
  35.4 5.5 %concatenate.18.keep_ref = f32[640,384]{1,0:T(8,128)} concatenate(f32[640,8]{1,0:T(8,128)S(1)} %get-tuple-element.82, f32[640,8]{1,0:T(8,128)S(1)} %get-tuple-element.82, f32[640,48]{1,0:T(8,128)S(1)} %broadcast_in_dim.78, f32[640,8]{1,0:T(8,128)S(1)} %get-tuple-element.82, f32[640,8]{1,0:T(8,128)S(1)} %get-tuple-element.82, f32[640,48]{1,0:T(8,128)S(1)} %broadcast_in_dim.78, ...), dimensions={1} | concatenate | bytes 1966080 | tf_op jit(solution)/shard_map/concatenate | solution.py:39
  40.9 1.2 copy-done.1
  42.1 1.2 copy-done.2
  43.3 1.2 copy-done.3
  44.5 1.2 copy-done.4
  45.7 1.9 copy-done.5
  47.6 38.6 %shard_map.245 = (bf16[640,512]{1,0:T(8,128)(2,1)S(1)}, bf16[640,1536]{1,0:T(8,128)(2,1)S(1)}, f32[1,1536]{1,0:T(1,128)S(1)}) custom-call(bf16[640,1024]{1,0:T(8,128)(2,1)S(1)} %fusion.14.ln_ref, bf16[640,1024]{1,0:T(8,128)(2,1)S(1)} %copy-done, bf16[1024,1536]{1,0:T(8,128)(2,1)S(1)} %copy-done.5, f32[1,1536]{1,0:T(1,128)S(1)} %reshape.90.bias_ref, ...), custom_call_target="tpu_custom_call" | custom-call | flops 12079595520 | bytes 16777216 | tf_op jit(solution)/shard_map/pallas_call | solution.py:149
  86.2 0.0 copy-start.19
  86.3 2.3 convolution_add_fusion.1
  88.6 1.5 copy-done.19
  90.1 6.6 %fusion.36 = (f32[2048]{0:T(1024)S(1)}, bf16[640,2048]{1,0:T(8,128)(2,1)S(1)}) fusion(f32[640,2048]{1,0:T(8,128)} %get-tuple-element.26, bf16[640,1024]{1,0:T(8,128)(2,1)S(1)} %copy-done, bf16[2048,1024]{1,0:T(8,128)(2,1)S(1)} %copy-done.19), kind=kOutput, calls=%fused_computation.62 | convolution fusion | flops 2698770432 | bytes 13377536 | tf_op jit(solution)/shard_map/dot_general | solution.py:69
  96.7 0.0 copy-start.8
  96.7 0.0 copy-start.20
  96.7 2.2 fusion.39
  99.0 0.0 copy-done.8
  99.0 1.3 copy-done.20
  100.2 5.0 %fusion.33 = (f32[1024]{0:T(1024)S(1)}, f32[1024]{0:T(1024)S(1)}, f32[640,1024]{1,0:T(8,128)}, f32[1024]{0:T(1024)S(1)}, f32[1024]{0:T(1024)S(1)}) fusion(f32[640]{0:T(1024)S(1)} %add_rsqrt_fusion, f32[640]{0:T(1024)S(1)} %broadcast_multiply_fusion.2, bf16[640,1024]{1,0:T(8,128)(2,1)S(1)} %copy-done.8, f32[1024]{0:T(1024)S(1)} %copy-done.22, ...), kind=kOutput, calls=%fused_computation.59 | convolution fusion | flops 2692214784 | bytes 13399040 | tf_op jit(solution)/shard_map/dot_general | solution.py:69
  105.2 2.3 convolution_bitcast_fusion.1
  107.6 2.9 copy.32
  110.5 0.0 reduce-scatter.13.cloned.1.call-update
  110.5 0.0 reduce-scatter.9.cloned.1.call-start
  110.6 6.2 %fusion.40 = f32[1024,1536]{1,0:T(8,128)} fusion(bf16[640,1024]{1,0:T(8,128)(2,1)S(1)} %fusion.14.ln_ref, bf16[640,1536]{1,0:T(8,128)(2,1)} %copy-done.6), kind=kOutput, calls=%fused_computation.66 | convolution fusion | flops 2013265920 | bytes 9568256 | tf_op jit(solution)/shard_map/dot_general | solution.py:57
  116.7 0.0 reduce-scatter.9.cloned.1.call-update
  116.8 0.0 reduce-scatter.11.cloned.1.call-start
  116.8 1.2 copy-done.9
  118.0 7.7 %fusion.30 = f32[1024,2048]{1,0:T(8,128)} fusion(bf16[640,2048]{1,0:T(8,128)(2,1)} %copy-done.25, bf16[640,1024]{1,0:T(8,128)(2,1)S(1)} %copy-done.9, f32[1024]{0:T(1024)S(1)} %copy-done.23, f32[1024]{0:T(1024)S(1)} %copy-done.22, f32[640]{0:T(1024)S(1)} %add_rsqrt_fusion, f32[640]{0:T(1024)S(1)} %broadcast_multiply_fusion.2), kind=kOutput, calls=%fused_computation.58 | convolution fusion | flops 2688286720 | bytes 12334080 | tf_op jit(solution)/shard_map/dot_general | solution.py:57
  125.8 0.0 reduce-scatter.11.cloned.1.call-update
  125.8 0.0 reduce-scatter.15.cloned.1.call-start
  125.8 7.9 %convolution_bitcast_fusion = f32[1024,2048]{0,1:T(8,128)} fusion(bf16[640,2048]{1,0:T(8,128)(2,1)} %copy-done.24, bf16[640,1024]{1,0:T(8,128)(2,1)S(1)} %copy-done), kind=kOutput, calls=%fused_computation.7 | convolution fusion | flops 2684354560 | bytes 12320768 | tf_op jit(solution)/shard_map/dot_general | solution.py:57
  133.7 9.3 %copy.34 = f32[1024,2048]{1,0:T(8,128)} copy(f32[1024,2048]{0,1:T(8,128)} %convolution_bitcast_fusion) | data formatting | bytes 16777216
  143.0 0.0 reduce-scatter.15.cloned.1.call-update
  143.0 3.1 collective-permute-start.1
  146.0 0.1 collective-permute-start
  146.2 0.1 broadcast_select_fusion
  146.3 0.1 select_bitcast_fusion
  146.4 57.7 %collective-permute-done.1 = f32[640,1024]{1,0:T(8,128)} collective-permute-done((f32[640,1024]{1,0:T(8,128)}, f32[640,1024]{1,0:T(8,128)}, u32[]{:S(2)}, u32[]{:S(2)}) %collective-permute-start.1) | collective-permute-done | bytes 2621472 | tf_op jit(solution)/shard_map/ppermute | solution.py:188
  204.1 3.5 fusion.35
  207.6 51.7 %collective-permute-done = f32[640,1024]{1,0:T(8,128)} collective-permute-done((f32[640,1024]{1,0:T(8,128)}, f32[640,1024]{1,0:T(8,128)}, u32[]{:S(2)}, u32[]{:S(2)}) %collective-permute-start) | collective-permute-done | bytes 2621472 | tf_op jit(solution)/shard_map/ppermute | solution.py:188
  259.3 4.1 convert_reduce_fusion.1
  263.4 41.5 %psum.7 = f32[12288]{0:T(1024)S(1)} all-reduce(f32[12288]{0:T(1024)S(1)} %constant_dynamic-update-slice_fusion), channel_id=1, replica_groups=mesh['dp'=16,'tensor'=2] {'dp','tensor'}, use_global_device_ids=true, to_apply=%region_10.0 | all-reduce | flops 12288 | bytes 98304 | tf_op jit(solution)/shard_map/psum | solution.py:259
  304.9 0.7 dynamic_slice.6
  305.5 0.6 dynamic_slice.7
  306.1 0.6 fusion.37
  306.7 0.0 reduce-scatter.9.cloned.1.call-done
  306.8 64.2 %reduce-scatter.11.cloned.1.call-done = f32[64,2048]{1,0:T(8,128)} async-done(((f32[1024,2048]{1,0:T(8,128)}), f32[64,2048]{1,0:T(8,128)}) %reduce-scatter.11.cloned.1.call-update) | async-done | bytes 524304 | tf_op jit(solution)/shard_map/reduce_scatter | solution.py:193
  370.9 107.6 %reduce-scatter.15.cloned.1.call-done = f32[64,2048]{1,0:T(8,128)} async-done(((f32[1024,2048]{1,0:T(8,128)}), f32[64,2048]{1,0:T(8,128)}) %reduce-scatter.15.cloned.1.call-update) | async-done | bytes 524304
  478.5 0.6 copy.46
  (54 shorter events, 0.3 us)
Async XLA Ops:
  7.2 3.4 copy-start.13
  7.2 299.6 %reduce-scatter.13.cloned.1.call-start = ((), (), s32[]{:S(2)}) async-start(), calls=%async_computation.6 | async-start | bytes 2228224
  16.8 4.9 %copy-start.7 = (bf16[640,1024]{1,0:T(8,128)(2,1)S(1)}, bf16[640,1024]{1,0:T(8,128)(2,1)}, u32[]{:S(2)}) copy-start(bf16[640,1024]{1,0:T(8,128)(2,1)} %param.14) | copy-start | bytes 3932164
  16.8 4.9 %copy-start.14 = (f32[1024]{0:T(1024)S(1)}, f32[1024]{0:T(1024)}, u32[]{:S(2)}) copy-start(f32[1024]{0:T(1024)} %param.17) | copy-start | bytes 12292
  16.8 4.9 %copy-start.15 = (f32[1024]{0:T(1024)S(1)}, f32[1024]{0:T(1024)}, u32[]{:S(2)}) copy-start(f32[1024]{0:T(1024)} %param.16) | copy-start | bytes 12292
  21.7 0.7 copy-start.21
  21.7 0.7 copy-start.22
  21.7 0.7 copy-start.23
  22.4 7.7 %copy-start.18 = (bf16[2048,1024]{1,0:T(8,128)(2,1)S(1)}, bf16[2048,1024]{1,0:T(8,128)(2,1)}, u32[]{:S(2)}) copy-start(bf16[2048,1024]{1,0:T(8,128)(2,1)} %param.26) | copy-start | bytes 12582916
  30.2 4.4 copy-start.24
  35.4 5.5 %copy-start = (bf16[640,1024]{1,0:T(8,128)(2,1)S(1)}, bf16[640,1024]{1,0:T(8,128)(2,1)}, u32[]{:S(2)}) copy-start(bf16[640,1024]{1,0:T(8,128)(2,1)} %up_ref.1) | copy-start | bytes 3932164
  40.9 1.2 copy-start.1
  42.1 1.2 copy-start.2
  43.3 1.2 copy-start.3
  44.5 1.2 copy-start.4
  45.7 1.9 copy-start.5
  47.6 38.6 %copy-start.11 = (f32[640,1024]{1,0:T(8,128)S(1)}, f32[640,1024]{1,0:T(8,128)}, u32[]{:S(2)}) copy-start(f32[640,1024]{1,0:T(8,128)} %fusion.38) | copy-start | bytes 7864324
  86.2 10.5 %copy-start.6 = (bf16[640,1536]{1,0:T(8,128)(2,1)}, bf16[640,1536]{1,0:T(8,128)(2,1)S(1)}, u32[]{:S(2)}) copy-start(bf16[640,1536]{1,0:T(8,128)(2,1)S(1)} %get-tuple-element.28) | copy-start | bytes 5898244
  86.2 3.8 copy-start.19
  96.7 2.3 copy-start.25
  96.7 2.3 copy-start.8
  96.7 3.5 copy-start.20
  110.5 196.2 %reduce-scatter.9.cloned.1.call-start = ((), (), s32[]{:S(2)}) async-start(), calls=%async_computation.4 | async-start | bytes 6684672 | tf_op jit(solution)/shard_map/reduce_scatter | solution.py:193
  116.7 1.3 copy-start.9
  116.8 254.2 %reduce-scatter.11.cloned.1.call-start = ((), (), s32[]{:S(2)}) async-start(), calls=%async_computation.5 | async-start | bytes 8912896 | tf_op jit(solution)/shard_map/reduce_scatter | solution.py:193
  125.8 352.7 %reduce-scatter.15.cloned.1.call-start = ((), (), s32[]{:S(2)}) async-start(), calls=%async_computation.7 | async-start | bytes 8912896
  143.0 61.1 %collective-permute-start.1 = (f32[640,1024]{1,0:T(8,128)}, f32[640,1024]{1,0:T(8,128)}, u32[]{:S(2)}, u32[]{:S(2)}) collective-permute-start(f32[640,1024]{1,0:T(8,128)} %get-tuple-element.69), channel_id=1, source_target_pairs={{0,1},{1,0},{2,3},{3,2},{4,5},{5,4},{6,7},{7,6},{8,9},{9,8},{10,11... | collective-permute-start | bytes 7864328 | tf_op jit(solution)/shard_map/ppermute | solution.py:188
  146.0 113.2 %collective-permute-start = (f32[640,1024]{1,0:T(8,128)}, f32[640,1024]{1,0:T(8,128)}, u32[]{:S(2)}, u32[]{:S(2)}) collective-permute-start(f32[640,1024]{1,0:T(8,128)} %convolution_add_fusion.1), channel_id=1, source_target_pairs={{0,1},{1,0},{2,3},{3,2},{4,5},{5,4},{6,7},{7,6},{8,9},{9,8},{10,11... | collective-permute-start | bytes 7864328 | tf_op jit(solution)/shard_map/ppermute | solution.py:188
  146.4 112.9 %copy-start.10 = (f32[640,1024]{1,0:T(8,128)S(1)}, f32[640,1024]{1,0:T(8,128)}, u32[]{:S(2)}) copy-start(f32[640,1024]{1,0:T(8,128)} %convolution_add_fusion.1) | copy-start | bytes 7864324
  146.4 112.9 %copy-start.16 = (f32[1024]{0:T(1024)S(1)}, f32[1024]{0:T(1024)}, u32[]{:S(2)}) copy-start(f32[1024]{0:T(1024)} %param.27) | copy-start | bytes 12292
  146.4 112.9 %copy-start.17 = (f32[1024]{0:T(1024)S(1)}, f32[1024]{0:T(1024)}, u32[]{:S(2)}) copy-start(f32[1024]{0:T(1024)} %param.23) | copy-start | bytes 12292
  306.7 172.4 %copy-start.12 = (f32[1024]{0:T(1024)}, f32[1024]{0:T(1024)S(1)}, u32[]{:S(2)}) copy-start(f32[1024]{0:T(1024)S(1)} %get-tuple-element.115) | copy-start | bytes 12292
Sparse Core Ops, SparseCore 0:
  110.6 64.5 reduce-scatter.12
  179.7 83.9 reduce-scatter.8
  268.4 102.4 reduce-scatter.10
  375.4 103.0 reduce-scatter.14
